TPU v7x, 32 devices: a whole 2x2x4 slice. The times are simulated.
32 devices in a mesh: prow: 4 (over z), pcol: 8 (over y, x, core).
Axes of the slice: x: 2, y: 2, z: 4, core: 2. Of those that a mesh axis runs over, the one named last changes fastest.
Arguments:
- anc_inverse: float32 [2048, 2048], P('pcol', 'prow')
- pattern_one: int32 [8, 4], replicated, may hold values from 0 to 7, as said below
- parents: int32 [8], replicated, may hold values from 0 to 7, as said below
- low_one: float32 [8, 1024, 256], P('pcol', 'prow'), may hold values from -2 to 2
- pivot_one: float32 [8, 256, 256], P('pcol'), may hold values from -4 to 4
- low_two: float32 [8, 1024, 256], P('pcol', 'prow'), may hold values from -2 to 2
- second_scaled_factor: float32 [8, 256, 256], P('pcol'), may hold values from -2 to 2
- second_pivot_inverse: float32 [8, 256, 256], P('pcol'), may hold values from -4 to 4
Outputs:
- column_one: float32 [8, 2048, 256], P('prow', 'pcol')
- diag_one: float32 [8, 256, 256], P('pcol')
- column_two: float32 [8, 2048, 256], P('prow', 'pcol')
- second_parent_inverse: float32 [8, 256, 256], P('pcol')
- second_diagonal_inverse: float32 [8, 256, 256], P('pcol')
Inputs may be any that keep to these rules, and one draw needn't show every extreme that they name: `pattern_one`: entry r of each row names an ancestor of process row r: it lies in r * 2 to r * 2 + 1; for each r, every ancestor of that range is entry r of exactly 4 rows. `parents`: every first-level supernode is the parent of exactly one second-level supernode.
All inputs are finite; a program needn't handle non-finite values.
Results may differ from a plain program's by a relative error of at most 0.000073.
Values sent between devices are 32-bit elements; how exact they have to be, the bound alone decides.
A program may use at most 128 MiB of HBM per device.

v0:
```python
import jax
import jax.numpy as jnp
from jax import lax
from jax.sharding import PartitionSpec as P


def batched(left, right):
    return jnp.einsum("kab,kbd->kad", left, right, precision=lax.Precision.HIGHEST)


def batched_left_t(left, right):
    return jnp.einsum("kba,kbd->kad", left, right, precision=lax.Precision.HIGHEST)


def pick_rows(hit_mask, count):
    total = hit_mask.shape[0]
    keys = jnp.where(hit_mask, 0, total).astype(jnp.int32) + jnp.arange(total, dtype=jnp.int32)
    chosen_rows = jnp.argsort(keys)[:count]
    valid = jnp.take(hit_mask, chosen_rows, axis=0).astype(jnp.float32)[:, None, None]
    return (chosen_rows, valid)


def body(
    anc_inverse,
    pattern_one,
    parents,
    low_one,
    pivot_one,
    low_two,
    second_scaled_factor,
    second_pivot_inverse,
):
    my_row = lax.axis_index("prow")
    my_col = lax.axis_index("pcol")
    row_count = lax.axis_size("prow")
    col_count = lax.axis_size("pcol")
    per_row_anc = col_count // row_count
    supernode_block_width = pivot_one.shape[1]
    per_col_one = pivot_one.shape[0]
    per_col_two = second_scaled_factor.shape[0]
    owned = anc_inverse.shape[1] // supernode_block_width
    zblocks = anc_inverse.reshape(supernode_block_width, owned, supernode_block_width).transpose(
        1, 0, 2
    )
    lowall = lax.all_gather(low_one, "pcol", axis=0, tiled=True)
    total_one = lowall.shape[0]
    owned_slot_list = lax.dynamic_index_in_dim(pattern_one, my_row, 1, keepdims=False)
    chosen = jnp.take(zblocks, owned_slot_list - my_row * owned, axis=0)
    first_terms = batched(chosen, lowall)
    lowsec, topall = (
        lax.all_gather(low_two, "pcol", axis=0, tiled=True),
        lax.all_gather(second_scaled_factor, "pcol", axis=0, tiled=True),
    )
    total_two = lowsec.shape[0]
    pattern_two = jnp.take(pattern_one, parents, axis=0)
    my_slots_two = lax.dynamic_index_in_dim(pattern_two, my_row, 1, keepdims=False)
    chosen_two = jnp.take(zblocks, my_slots_two - my_row * owned, axis=0)
    first_full = -lax.psum(first_terms, "prow")
    share = total_two // row_count
    start = my_row * share
    parents_share = lax.dynamic_slice_in_dim(parents, start, share, 0)
    tops_share = lax.dynamic_slice_in_dim(topall, start, share, 0)
    carried = batched(jnp.take(first_full, parents_share, axis=0), tops_share)
    base_terms = batched(chosen_two, lowsec)
    updated = lax.dynamic_slice_in_dim(base_terms, start, share, 0) + carried
    second_terms = lax.dynamic_update_slice_in_dim(base_terms, updated, start, 0)
    second_full = -lax.psum(second_terms, "prow")
    rows_one, valid_one = pick_rows(owned_slot_list == my_col, total_one // per_row_anc)
    pivot_small = valid_one * batched_left_t(
        jnp.take(lowall, rows_one, axis=0), jnp.take(first_full, rows_one, axis=0)
    )
    pivot_terms = jnp.zeros_like(first_full).at[rows_one].add(pivot_small)
    pivot_part = lax.psum_scatter(pivot_terms, "pcol", scatter_dimension=0, tiled=True)
    pivot_sum = lax.psum(pivot_part, "prow")
    diag_one = pivot_one - pivot_sum
    count_one = first_full.shape[0] // row_count
    column_one = lax.dynamic_slice_in_dim(first_full, my_row * count_one, count_one, 0)
    second_level_count = second_full.shape[0] // row_count
    column_two = lax.dynamic_slice_in_dim(
        second_full, my_row * second_level_count, second_level_count, 0
    )
    rows_two, valid_two = pick_rows(my_slots_two == my_col, total_two // per_row_anc)
    lows_picked = jnp.take(lowsec, rows_two, axis=0)
    parent_picked = jnp.take(first_full, jnp.take(parents, rows_two, axis=0), axis=0)
    cross_small = valid_two * batched_left_t(parent_picked, lows_picked)
    diag_small = valid_two * batched_left_t(lows_picked, jnp.take(second_full, rows_two, axis=0))
    local_parent = parents - my_col * per_col_one
    own_parent = (local_parent >= 0) & (local_parent < per_col_one)
    rows_own, valid_own = pick_rows(own_parent, per_col_two)
    valid_own = valid_own * (my_row == 0).astype(jnp.float32)
    local_picked = jnp.clip(jnp.take(local_parent, rows_own, axis=0), 0, per_col_one - 1)
    picked = jnp.take(diag_one, local_picked, axis=0)
    own_small = valid_own * batched(picked, jnp.take(topall, rows_own, axis=0))
    cross_terms = (
        jnp.zeros_like(second_full).at[rows_two].add(cross_small).at[rows_own].add(own_small)
    )
    diag_terms = jnp.zeros_like(second_full).at[rows_two].add(diag_small)
    part_cross, part_diag = (
        lax.psum_scatter(cross_terms, "pcol", scatter_dimension=0, tiled=True),
        lax.psum_scatter(diag_terms, "pcol", scatter_dimension=0, tiled=True),
    )
    sum_cross, sum_diag = lax.psum((part_cross, part_diag), "prow")
    second_parent_inverse = -sum_cross
    second_diagonal_inverse = (
        second_pivot_inverse
        - batched_left_t(second_scaled_factor, second_parent_inverse)
        - sum_diag
    )
    return (column_one, diag_one, column_two, second_parent_inverse, second_diagonal_inverse)


def solution(mesh):
    placed = (
        P("pcol", "prow"),
        P(),
        P(),
        P("pcol", "prow", None),
        P("pcol", None, None),
        P("pcol", "prow", None),
        P("pcol", None, None),
        P("pcol", None, None),
    )
    return jax.shard_map(
        body,
        mesh=mesh,
        in_specs=placed,
        out_specs=(
            P("prow", "pcol", None),
            P("pcol", None, None),
            P("prow", "pcol", None),
            P("pcol", None, None),
            P("pcol", None, None),
        ),
        check_vma=False,
    )
```

profile of v0, /device:TPU:0, one launch (start us, length us, event | category | flops | bytes accessed | tf_op | source)
XLA Modules:
  0.0 471.5 jit_solution(3958737760766188225)
XLA Ops:
  7.2 0.7 all-gather.4.cloned.1.call-update
  8.0 1.2 copy.34
  9.7 0.7 gather_fusion.3
  10.5 30.0 %all-gather.4.cloned.1.call-done = f32[8,256,256]{2,1,0:T(8,128)} async-done(((f32[1,256,256]{2,1,0:T(8,128)}), f32[8,256,256]{2,1,0:T(8,128)}) %all-gather.4.cloned.1.call-update) | async-done | bytes 2097168 | tf_op jit(solution)/shard_map/all_gather | solution.py:45
  40.4 5.1 %fusion.2 = f32[8,256,256]{2,1,0:T(8,128)} fusion(f32[8,256,256]{2,1,0:T(8,128)} %all-gather.4.cloned.1.call-done, f32[8,256,256]{2,1,0:T(8,128)S(1)} %gather_fusion.3, pred[8]{0:T(512)(128)(4,1)S(1)} %compare_and_fusion.4), kind=kOutput, calls=%fused_computation.17 | convolution fusion | flops 1611137024 | bytes 6291464 | tf_op jit(solution)/shard_map/kab,kbd->kad/dot_general | solution.py:8
  45.6 0.7 all-gather.6.cloned.1.call-update
  47.1 1.0 sort.45
  48.1 0.6 gather_fusion.4
  48.7 1.7 gather_fusion.5
  50.4 81.4 %all-reduce.6.cloned.1.call-done = f32[8,256,256]{2,1,0:T(8,128)} async-done(((f32[8,256,256]{2,1,0:T(8,128)}), f32[8,256,256]{2,1,0:T(8,128)}) %all-reduce.6.cloned.1.call-update) | async-done | bytes 2097168 | tf_op jit(solution)/shard_map/psum | solution.py:58
  131.8 1.8 neg.9
  133.6 1.7 gather_fusion.6
  135.3 4.5 convolution_multiply_fusion.2
  140.0 2.3 scatter_fusion
  142.3 1.3 copy-done.3
  144.8 2.0 gather_fusion.7
  146.9 13.7 %all-gather.6.cloned.1.call-done = f32[8,256,256]{2,1,0:T(8,128)} async-done(((f32[1,256,256]{2,1,0:T(8,128)}), f32[8,256,256]{2,1,0:T(8,128)}) %all-gather.6.cloned.1.call-update) | async-done | bytes 2097168 | tf_op jit(solution)/shard_map/all_gather | solution.py:51
  160.6 5.8 %fusion = f32[8,256,256]{2,1,0:T(8,128)} fusion(f32[8,256,256]{2,1,0:T(8,128)} %all-gather.6.cloned.1.call-done, f32[8,256,256]{2,1,0:T(8,128)} %gather_fusion.7, pred[8]{0:T(512)(128)(4,1)S(1)} %compare_and_fusion.2), kind=kOutput, calls=%fused_computation.15 | convolution fusion | flops 1611137024 | bytes 6291464 | tf_op jit(solution)/shard_map/kab,kbd->kad/dot_general | solution.py:8
  166.9 23.2 %all-gather.8.cloned.1.call-done = f32[8,256,256]{2,1,0:T(8,128)} async-done(((f32[1,256,256]{2,1,0:T(8,128)}), f32[8,256,256]{2,1,0:T(8,128)}) %all-gather.8.cloned.1.call-update) | async-done | bytes 2097168 | tf_op jit(solution)/shard_map/all_gather | solution.py:52
  190.1 2.7 fusion.4
  192.9 41.5 %reduce-scatter.4.cloned.1.call-done = f32[1,256,256]{2,1,0:T(8,128)} async-done(((f32[8,256,256]{2,1,0:T(8,128)}), f32[1,256,256]{2,1,0:T(8,128)}) %reduce-scatter.4.cloned.1.call-update) | async-done | bytes 262160 | tf_op jit(solution)/shard_map/reduce_scatter | solution.py:73
  234.7 1.0 sort.46
  235.6 0.6 gather_fusion.2
  236.3 0.6 gather_fusion.8
  236.9 1.0 sort.47
  238.0 0.6 dynamic-slice.18
  240.5 0.7 and_reduce_fusion
  241.2 2.6 gather_fusion.10
  243.8 1.6 gather_fusion.9
  245.3 4.2 convolution_multiply_fusion.1
  249.8 2.3 scatter_fusion.1
  252.1 79.3 %all-reduce.10.cloned.1.call-done = (f32[1,256,256]{2,1,0:T(8,128)}, f32[8,256,256]{2,1,0:T(8,128)}) async-done(((f32[1,256,256]{2,1,0:T(8,128)}, f32[8,256,256]{2,1,0:T(8,128)}), (f32[1,256,256]{2,1,0:T(8,128)}, f32[8,256,256]{2,1,0:T(8,128)})) %all-reduce.10.cloned.1.call-update) | async-done | bytes 2359312 | tf_op jit(solution)/shard_map/psum | solution.py:74
  331.4 1.1 sub.32
  332.5 2.0 fusion.8
  334.5 1.3 copy-done.1
  335.9 1.8 neg.10
  337.7 1.7 gather_fusion.11
  339.4 4.3 convolution_multiply_fusion
  343.9 1.1 copy-done.8
  345.0 1.2 scatter_fusion.2
  346.2 1.3 copy-done.2
  347.7 28.5 %reduce-scatter.6.cloned.1.call-done = f32[1,256,256]{2,1,0:T(8,128)} async-done(((f32[8,256,256]{2,1,0:T(8,128)}), f32[1,256,256]{2,1,0:T(8,128)}) %reduce-scatter.6.cloned.1.call-update) | async-done | bytes 262160 | tf_op jit(solution)/shard_map/reduce_scatter | solution.py:99
  376.2 44.4 %reduce-scatter.8.cloned.1.call-done = f32[1,256,256]{2,1,0:T(8,128)} async-done(((f32[8,256,256]{2,1,0:T(8,128)}), f32[1,256,256]{2,1,0:T(8,128)}) %reduce-scatter.8.cloned.1.call-update) | async-done | bytes 262160 | tf_op jit(solution)/shard_map/reduce_scatter | solution.py:100
  420.6 1.9 constant_dynamic-slice_fusion.1
  422.5 1.9 constant_dynamic-slice_fusion
  424.3 37.3 %all-reduce.8.cloned.1.call-done = (f32[1,256,256]{2,1,0:T(8,128)}, f32[1,256,256]{2,1,0:T(8,128)}) async-done(((f32[1,256,256]{2,1,0:T(8,128)}, f32[1,256,256]{2,1,0:T(8,128)}), (f32[1,256,256]{2,1,0:T(8,128)}, f32[1,256,256]{2,1,0:T(8,128)})) %all-reduce.8.cloned.1.call-update) | async-done | bytes 524304 | tf_op jit(solution)/shard_map/psum | solution.py:102
  461.6 1.0 neg.11
  462.6 2.3 fusion.10
  (77 shorter events, 4.8 us)
Async XLA Ops:
  7.2 2.3 copy-start.13
  7.2 2.5 copy-start
  7.2 33.2 %all-gather.4.cloned.1.call-start = ((), (), s32[]{:S(2)}) async-start(), calls=%async_computation.3 | async-start | bytes 2359296 | tf_op jit(solution)/shard_map/all_gather | solution.py:45
  7.9 123.9 %all-reduce.6.cloned.1.call-start = ((), (), s32[]{:S(2)}) async-start(), calls=%async_computation.4 | async-start | bytes 4194304 | tf_op jit(solution)/shard_map/psum | solution.py:58
  45.5 3.2 copy-start.7
  45.5 115.0 %all-gather.6.cloned.1.call-start = ((), (), s32[]{:S(2)}) async-start(), calls=%async_computation.6 | async-start | bytes 2359296 | tf_op jit(solution)/shard_map/all_gather | solution.py:51
  46.3 143.9 %all-gather.8.cloned.1.call-start = ((), (), s32[]{:S(2)}) async-start(), calls=%async_computation.7 | async-start | bytes 2359296 | tf_op jit(solution)/shard_map/all_gather | solution.py:52
  46.9 187.5 %reduce-scatter.4.cloned.1.call-start = ((), (), s32[]{:S(2)}) async-start(), calls=%async_computation.5 | async-start | bytes 2359296 | tf_op jit(solution)/shard_map/reduce_scatter | solution.py:73
  133.6 1.7 copy-start.4
  142.3 1.3 copy-start.3
  143.7 187.7 %all-reduce.10.cloned.1.call-start = ((), (), s32[]{:S(2)}) async-start(), calls=%async_computation.11 | async-start | bytes 4718592 | tf_op jit(solution)/shard_map/psum | solution.py:74
  146.9 19.5 %copy-start.5 = (f32[8,256,256]{2,1,0:T(8,128)S(1)}, f32[8,256,256]{2,1,0:T(8,128)}, u32[]{:S(2)}) copy-start(f32[8,256,256]{2,1,0:T(8,128)} %copy-done.4) | copy-start | bytes 6291460
  192.9 47.6 %copy-start.14 = (s32[3]{0:T(128)S(1)}, s32[3]{0:T(128)}, u32[]{:S(2)}) copy-start(s32[3]{0:T(128)} %constant.171.clone.1) | copy-start | bytes 40
  234.4 141.8 %reduce-scatter.6.cloned.1.call-start = ((), (), s32[]{:S(2)}) async-start(), calls=%async_computation.8 | async-start | bytes 2359296 | tf_op jit(solution)/shard_map/reduce_scatter | solution.py:99
  332.5 5.2 %copy-start.9 = (f32[1,256,256]{2,1,0:T(8,128)}, f32[1,256,256]{2,1,0:T(8,128)S(1)}, u32[]{:S(2)}) copy-start(f32[1,256,256]{2,1,0:T(8,128)S(1)} %sub.32) | copy-start | bytes 786436
  334.5 1.3 copy-start.1
  335.9 84.7 %reduce-scatter.8.cloned.1.call-start = ((), (), s32[]{:S(2)}) async-start(), calls=%async_computation.9 | async-start | bytes 2359296 | tf_op jit(solution)/shard_map/reduce_scatter | solution.py:100
  337.7 1.7 copy-start.6
  343.7 1.3 copy-start.8
  346.2 1.3 copy-start.2
  347.6 115.0 %copy-start.10 = (f32[1,256,256]{2,1,0:T(8,128)S(1)}, f32[1,256,256]{2,1,0:T(8,128)}, u32[]{:S(2)}) copy-start(f32[1,256,256]{2,1,0:T(8,128)} %param.22) | copy-start | bytes 786436
  347.6 115.0 %copy-start.12 = (f32[1,256,256]{2,1,0:T(8,128)S(1)}, f32[1,256,256]{2,1,0:T(8,128)}, u32[]{:S(2)}) copy-start(f32[1,256,256]{2,1,0:T(8,128)} %param.23) | copy-start | bytes 786436
  347.6 114.0 %all-reduce.8.cloned.1.call-start = ((), (), s32[]{:S(2)}) async-start(), calls=%async_computation.10 | async-start | bytes 1048576 | tf_op jit(solution)/shard_map/psum | solution.py:102
  462.6 2.4 copy-start.11
Sparse Core Ops, SparseCore 0:
  9.9 30.4 all-gather.3
  45.7 86.1 all-reduce.5
  133.7 26.8 all-gather.5
  162.3 27.7 all-gather.7
  193.3 41.0 reduce-scatter.3
  236.7 94.6 all-reduce.9
  336.0 40.1 reduce-scatter.5
  379.5 41.0 reduce-scatter.7
  423.0 38.6 all-reduce.7
where the time goes:
time: 472 us
  waiting for transfers between devices  381 us (81%)
  matrix products  31 us (7%)
  local copies, waits for them, and re-layouts  27 us (6%)
  other arithmetic  16 us (3%)
  between operations  15.6 us (3%)
    psum x1, waiting for transfers between devices, body(): first_full = -lax.psum(first_terms, 'prow')  81.4 us
    psum x1, waiting for transfers between devices, body(): pivot_sum = lax.psum(pivot_part, 'prow')  79.3 us
    reduce_scatter x1, waiting for transfers between devices, body(): lax.psum_scatter(diag_terms, 'pcol', scatter_dimension=0, tiled=True)  44.4 us
    reduce_scatter x1, waiting for transfers between devices, body(): lax.psum_scatter(pivot_terms, 'pcol', scatter_dimension=0, tiled=True)  41.5 us
    psum x1, waiting for transfers between devices, body(): sum_cross, sum_diag = lax.psum((part_cross, part_diag), 'prow')  37.3 us
    all_gather x1, waiting for transfers between devices, body(): lowall = lax.all_gather(low_one, 'pcol', axis=0, tiled=True)  30 us
    reduce_scatter x1, waiting for transfers between devices, body(): lax.psum_scatter(cross_terms, 'pcol', scatter_dimension=0, tiled=True)  28.5 us
    all_gather x1, waiting for transfers between devices, body(): lax.all_gather(second_scaled_factor, 'pcol', axis=0, tiled=True)  23.2 us
  transfers between devices with their start and end apart: 9, of which 9 were waited for; matrix products, arithmetic and copies ran while one was open for 12% of the time, Pallas kernels for 0%

commit v1 on v0

--- a/solution.py
+++ b/solution.py
@@ -2,6 +2,12 @@
 import jax.numpy as jnp
 from jax import lax
 from jax.sharding import PartitionSpec as P
+
+
+def summed_here(shard, name):
+    parts = lax.all_gather(shard, name, axis=0, tiled=False)
+    acc = parts.sum(axis=0)
+    return acc
 
 
 def batched(left, right):
@@ -55,7 +61,7 @@
     pattern_two = jnp.take(pattern_one, parents, axis=0)
     my_slots_two = lax.dynamic_index_in_dim(pattern_two, my_row, 1, keepdims=False)
     chosen_two = jnp.take(zblocks, my_slots_two - my_row * owned, axis=0)
-    first_full = -lax.psum(first_terms, "prow")
+    first_full = -summed_here(first_terms, "prow")
     share = total_two // row_count
     start = my_row * share
     parents_share = lax.dynamic_slice_in_dim(parents, start, share, 0)

time: 472 us -> 535 us (1.13)
  waiting for transfers between devices: 381 us -> 438 us
  other arithmetic: 16 us -> 21.7 us
    all_gather x0 -> x1, waiting for transfers between devices: none -> 145 us  [summed_here(): parts = lax.all_gather(shard, name, axis=0, tiled=False)]
    psum x1 -> x0, waiting for transfers between devices: 81.4 us -> none  [body(): first_full = -lax.psum(first_terms, 'prow')]
    all_gather x1, waiting for transfers between devices: 13.7 us -> 7.1 us  [body(): lax.all_gather(low_two, 'pcol', axis=0, tiled=True)]
    reduce_sum x0 -> x1, other arithmetic: none -> 5.59 us  [summed_here(): acc = parts.sum(axis=0)]
where the time goes in v1:
time: 535 us; the launch traced here: 534 us
  waiting for transfers between devices  438 us (82%)
  matrix products  30.9 us (6%)
  local copies, waits for them, and re-layouts  27.1 us (5%)
  other arithmetic  21.7 us (4%)
  between operations  15.6 us (3%)
    all_gather x1, waiting for transfers between devices, summed_here(): parts = lax.all_gather(shard, name, axis=0, tiled=False)  145 us
    psum x1, waiting for transfers between devices, body(): pivot_sum = lax.psum(pivot_part, 'prow')  79.3 us
    reduce_scatter x1, waiting for transfers between devices, body(): lax.psum_scatter(diag_terms, 'pcol', scatter_dimension=0, tiled=True)  44.4 us
    reduce_scatter x1, waiting for transfers between devices, body(): lax.psum_scatter(pivot_terms, 'pcol', scatter_dimension=0, tiled=True)  41.6 us
    psum x1, waiting for transfers between devices, body(): sum_cross, sum_diag = lax.psum((part_cross, part_diag), 'prow')  37.3 us
    all_gather x1, waiting for transfers between devices, body(): lowall = lax.all_gather(low_one, 'pcol', axis=0, tiled=True)  30 us
    reduce_scatter x1, waiting for transfers between devices, body(): lax.psum_scatter(cross_terms, 'pcol', scatter_dimension=0, tiled=True)  28.5 us
    all_gather x1, waiting for transfers between devices, body(): lax.all_gather(second_scaled_factor, 'pcol', axis=0, tiled=True)  23.3 us
  transfers between devices with their start and end apart: 9, of which 9 were waited for; matrix products, arithmetic and copies ran while one was open for 12% of the time, Pallas kernels for 0%

profile of v1, /device:TPU:0, one launch (start us, length us, event | category | flops | bytes accessed | tf_op | source)
XLA Modules:
  0.0 534.2 jit_solution(9116349264523007068)
XLA Ops:
  7.2 0.7 all-gather.6.cloned.1.call-update
  8.0 1.2 copy.34
  9.7 0.7 gather_fusion.3
  10.5 30.0 %all-gather.6.cloned.1.call-done = f32[8,256,256]{2,1,0:T(8,128)} async-done(((f32[1,256,256]{2,1,0:T(8,128)}), f32[8,256,256]{2,1,0:T(8,128)}) %all-gather.6.cloned.1.call-update) | async-done | bytes 2097168 | tf_op jit(solution)/shard_map/all_gather | solution.py:51
  40.4 5.1 fusion.2
  45.6 0.7 all-gather.8.cloned.1.call-update
  47.1 1.0 sort.45
  48.1 0.6 gather_fusion.4
  48.8 1.6 gather_fusion.5
  50.3 145.0 %all-gather.12.cloned.1.call-done = f32[32,256,256]{2,1,0:T(8,128)} async-done(((f32[8,256,256]{2,1,0:T(8,128)}), f32[32,256,256]{2,1,0:T(8,128)}) %all-gather.12.cloned.1.call-update) | async-done | bytes 8388624 | tf_op jit(solution)/shard_map/all_gather | solution.py:8
  195.4 5.6 %reduce_sum.9 = f32[8,256,256]{2,1,0:T(8,128)} reduce(f32[4,8,256,256]{3,2,1,0:T(8,128)} %bitcast.42, f32[]{:T(128)} %constant.163.clone.1), dimensions={0}, to_apply=%region_0.2 | reduce | flops 1572864 | bytes 10485764 | tf_op jit(solution)/shard_map/reduce_sum | solution.py:9
  200.9 1.8 neg.9
  202.8 1.8 gather_fusion.6
  204.6 4.5 convolution_multiply_fusion.2
  209.3 2.3 scatter_fusion
  211.6 1.3 copy-done.3
  214.0 2.0 gather_fusion.7
  216.2 7.1 %all-gather.8.cloned.1.call-done = f32[8,256,256]{2,1,0:T(8,128)} async-done(((f32[1,256,256]{2,1,0:T(8,128)}), f32[8,256,256]{2,1,0:T(8,128)}) %all-gather.8.cloned.1.call-update) | async-done | bytes 2097168 | tf_op jit(solution)/shard_map/all_gather | solution.py:57
  223.3 5.7 %fusion = f32[8,256,256]{2,1,0:T(8,128)} fusion(f32[8,256,256]{2,1,0:T(8,128)} %all-gather.8.cloned.1.call-done, f32[8,256,256]{2,1,0:T(8,128)} %gather_fusion.7, pred[8]{0:T(512)(128)(4,1)S(1)} %compare_and_fusion.2), kind=kOutput, calls=%fused_computation.15 | convolution fusion | flops 1611137024 | bytes 6291464 | tf_op jit(solution)/shard_map/kab,kbd->kad/dot_general | solution.py:14
  229.6 23.3 %all-gather.10.cloned.1.call-done = f32[8,256,256]{2,1,0:T(8,128)} async-done(((f32[1,256,256]{2,1,0:T(8,128)}), f32[8,256,256]{2,1,0:T(8,128)}) %all-gather.10.cloned.1.call-update) | async-done | bytes 2097168 | tf_op jit(solution)/shard_map/all_gather | solution.py:58
  252.8 2.7 fusion.4
  255.5 41.6 %reduce-scatter.4.cloned.1.call-done = f32[1,256,256]{2,1,0:T(8,128)} async-done(((f32[8,256,256]{2,1,0:T(8,128)}), f32[1,256,256]{2,1,0:T(8,128)}) %reduce-scatter.4.cloned.1.call-update) | async-done | bytes 262160 | tf_op jit(solution)/shard_map/reduce_scatter | solution.py:79
  297.3 1.0 sort.46
  298.3 0.6 gather_fusion.2
  298.9 0.6 gather_fusion.8
  299.6 1.0 sort.47
  303.1 0.7 and_reduce_fusion
  303.8 2.6 gather_fusion.10
  306.4 1.6 gather_fusion.9
  308.1 4.2 convolution_multiply_fusion.1
  312.4 2.3 scatter_fusion.1
  314.8 79.3 %all-reduce.7.cloned.1.call-done = (f32[1,256,256]{2,1,0:T(8,128)}, f32[8,256,256]{2,1,0:T(8,128)}) async-done(((f32[1,256,256]{2,1,0:T(8,128)}, f32[8,256,256]{2,1,0:T(8,128)}), (f32[1,256,256]{2,1,0:T(8,128)}, f32[8,256,256]{2,1,0:T(8,128)})) %all-reduce.7.cloned.1.call-update) | async-done | bytes 2359312 | tf_op jit(solution)/shard_map/psum | solution.py:80
  394.1 1.1 sub.32
  395.2 2.0 fusion.8
  397.2 1.3 copy-done.1
  398.6 1.8 neg.10
  400.4 1.7 gather_fusion.11
  402.1 4.3 convolution_multiply_fusion
  406.6 1.1 copy-done.8
  407.7 1.2 scatter_fusion.2
  408.9 1.3 copy-done.2
  410.3 28.5 %reduce-scatter.6.cloned.1.call-done = f32[1,256,256]{2,1,0:T(8,128)} async-done(((f32[8,256,256]{2,1,0:T(8,128)}), f32[1,256,256]{2,1,0:T(8,128)}) %reduce-scatter.6.cloned.1.call-update) | async-done | bytes 262160 | tf_op jit(solution)/shard_map/reduce_scatter | solution.py:105
  438.8 44.4 %reduce-scatter.8.cloned.1.call-done = f32[1,256,256]{2,1,0:T(8,128)} async-done(((f32[8,256,256]{2,1,0:T(8,128)}), f32[1,256,256]{2,1,0:T(8,128)}) %reduce-scatter.8.cloned.1.call-update) | async-done | bytes 262160 | tf_op jit(solution)/shard_map/reduce_scatter | solution.py:106
  483.3 1.9 constant_dynamic-slice_fusion.1
  485.2 1.9 constant_dynamic-slice_fusion
  487.0 37.3 %all-reduce.5.cloned.1.call-done = (f32[1,256,256]{2,1,0:T(8,128)}, f32[1,256,256]{2,1,0:T(8,128)}) async-done(((f32[1,256,256]{2,1,0:T(8,128)}, f32[1,256,256]{2,1,0:T(8,128)}), (f32[1,256,256]{2,1,0:T(8,128)}, f32[1,256,256]{2,1,0:T(8,128)})) %all-reduce.5.cloned.1.call-update) | async-done | bytes 524304 | tf_op jit(solution)/shard_map/psum | solution.py:108
  524.3 1.0 neg.11
  525.3 2.3 fusion.10
  (78 shorter events, 5.4 us)
Async XLA Ops:
  7.2 2.3 copy-start.13
  7.2 2.5 copy-start
  7.2 33.2 %all-gather.6.cloned.1.call-start = ((), (), s32[]{:S(2)}) async-start(), calls=%async_computation.3 | async-start | bytes 2359296 | tf_op jit(solution)/shard_map/all_gather | solution.py:51
  7.9 187.4 %all-gather.12.cloned.1.call-start = ((), (), s32[]{:S(2)}) async-start(), calls=%async_computation.9 | async-start | bytes 10485760 | tf_op jit(solution)/shard_map/all_gather | solution.py:8
  45.5 3.2 copy-start.7
  45.6 177.7 %all-gather.8.cloned.1.call-start = ((), (), s32[]{:S(2)}) async-start(), calls=%async_computation.5 | async-start | bytes 2359296 | tf_op jit(solution)/shard_map/all_gather | solution.py:57
  46.3 206.5 %all-gather.10.cloned.1.call-start = ((), (), s32[]{:S(2)}) async-start(), calls=%async_computation.6 | async-start | bytes 2359296 | tf_op jit(solution)/shard_map/all_gather | solution.py:58
  46.9 250.2 %reduce-scatter.4.cloned.1.call-start = ((), (), s32[]{:S(2)}) async-start(), calls=%async_computation.4 | async-start | bytes 2359296 | tf_op jit(solution)/shard_map/reduce_scatter | solution.py:79
  202.8 1.8 copy-start.4
  211.6 1.3 copy-start.3
  212.9 181.2 %all-reduce.7.cloned.1.call-start = ((), (), s32[]{:S(2)}) async-start(), calls=%async_computation.11 | async-start | bytes 4718592 | tf_op jit(solution)/shard_map/psum | solution.py:80
  216.1 12.8 %copy-start.5 = (f32[8,256,256]{2,1,0:T(8,128)S(1)}, f32[8,256,256]{2,1,0:T(8,128)}, u32[]{:S(2)}) copy-start(f32[8,256,256]{2,1,0:T(8,128)} %copy-done.4) | copy-start | bytes 6291460
  255.5 47.6 %copy-start.14 = (s32[3]{0:T(128)S(1)}, s32[3]{0:T(128)}, u32[]{:S(2)}) copy-start(s32[3]{0:T(128)} %constant.172.clone.1) | copy-start | bytes 40
  297.1 141.8 %reduce-scatter.6.cloned.1.call-start = ((), (), s32[]{:S(2)}) async-start(), calls=%async_computation.7 | async-start | bytes 2359296 | tf_op jit(solution)/shard_map/reduce_scatter | solution.py:105
  395.2 5.2 copy-start.9
  397.2 1.3 copy-start.1
  398.6 84.7 %reduce-scatter.8.cloned.1.call-start = ((), (), s32[]{:S(2)}) async-start(), calls=%async_computation.8 | async-start | bytes 2359296 | tf_op jit(solution)/shard_map/reduce_scatter | solution.py:106
  400.4 1.7 copy-start.6
  406.4 1.3 copy-start.8
  408.9 1.3 copy-start.2
  410.3 115.0 %copy-start.10 = (f32[1,256,256]{2,1,0:T(8,128)S(1)}, f32[1,256,256]{2,1,0:T(8,128)}, u32[]{:S(2)}) copy-start(f32[1,256,256]{2,1,0:T(8,128)} %param.22) | copy-start | bytes 786436
  410.3 115.0 %copy-start.12 = (f32[1,256,256]{2,1,0:T(8,128)S(1)}, f32[1,256,256]{2,1,0:T(8,128)}, u32[]{:S(2)}) copy-start(f32[1,256,256]{2,1,0:T(8,128)} %param.23) | copy-start | bytes 786436
  410.3 114.0 %all-reduce.5.cloned.1.call-start = ((), (), s32[]{:S(2)}) async-start(), calls=%async_computation.10 | async-start | bytes 1048576 | tf_op jit(solution)/shard_map/psum | solution.py:108
  525.3 2.4 copy-start.11
Sparse Core Ops, SparseCore 0:
  9.9 30.4 all-gather.5
  45.7 149.6 all-gather.11
  197.2 25.9 all-gather.7
  225.0 27.7 all-gather.9
  255.9 41.0 reduce-scatter.3
  299.4 94.6 all-reduce.6
  398.7 40.1 reduce-scatter.5
  442.1 41.0 reduce-scatter.7
  485.7 38.6 all-reduce.4
